TPU v7x, 512 devices: a whole 4x4x16 slice. The times are simulated.
512 devices in a mesh: row: 16 (over y_hi, x, core), col: 32 (over y_lo, z).
Axes of the slice: x: 4, y: 4 (y_hi: 2, y_lo: 2; y = y_hi * 2 + y_lo), z: 16, core: 2. Of those that a mesh axis runs over, the one named last changes fastest.
Arguments:
- inputs: bfloat16 [256, 512, 256], P('row', 'col'), may hold values from -6 to 6
- stored: bfloat16 [256, 512, 256], P('row', 'col'), may hold values from -6 to 6
- upstream: bfloat16 [256, 512, 256], P('row', 'col'), may hold values from -6 to 6
- weight_in: bfloat16 [256, 1024], replicated, may hold values from -0.375 to 0.375
- weight_out: bfloat16 [1024, 256], replicated, may hold values from -0.1875 to 0.1875
- kernel: bfloat16 [27, 27, 256], replicated, may hold values from -0.21875 to 0.21875
Outputs:
- grad_inputs: bfloat16 [256, 512, 256], P('row', 'col')
- grad_weight_in: bfloat16 [256, 1024], replicated
- grad_weight_out: bfloat16 [1024, 256], replicated
- grad_kernel: bfloat16 [27, 27, 256], replicated
All inputs are finite; a program needn't handle non-finite values.
Results may differ from a plain program's by a relative error of at most 0.0052.
Values may be sent and summed in bfloat16 or wider, within the bound.
No kernel may reach another device: no remote copies, remote signals or barrier semaphores. Data moves between devices by JAX's collectives and lax.ppermute only.
A program may use at most 64 MiB of HBM per device.

v0:
```python
import math
import jax
import jax.numpy as jnp
from jax import lax
from jax.sharding import PartitionSpec as P

KS = 27
gelu_coef = 0.044715
root_coef = math.sqrt(2.0 / math.pi)


def padded_2(block, sides, width):
    for axis, dim in sides:
        count = lax.axis_size(axis)
        forward = [(i, i + 1) for i in range(count - 1)]
        backward = [(target, source) for source, target in forward]
        low = lax.ppermute(
            lax.slice_in_dim(block, block.shape[dim] - width, None, axis=dim), axis, forward
        )
        high = lax.ppermute(lax.slice_in_dim(block, 0, width, axis=dim), axis, backward)
        block = jnp.concatenate([low, block, high], axis=dim)
    return block


def gelu_parts(values):
    tanh_part = jnp.tanh(root_coef * (values + gelu_coef * values * values * values))
    result = 0.5 * values * (1.0 + tanh_part)
    slopes = 0.5 * (1.0 + tanh_part) + 0.5 * values * (1.0 - tanh_part * tanh_part) * root_coef * (
        1.0 + 3.0 * gelu_coef * values * values
    )
    return (result, slopes)


def per_device(inputs, stored, upstream, weight_in, weight_out, kernel):
    tile_rows, tile_cols, channels = stored.shape
    radius = KS // 2
    padded_in = padded_2(inputs, (("row", 0), ("col", 1)), radius)
    flat_z = stored.reshape(tile_rows * tile_cols, channels)
    flat_g = upstream.reshape(tile_rows * tile_cols, channels)
    hidden = jnp.dot(flat_z, weight_in, preferred_element_type=jnp.float32)
    values, slopes = gelu_parts(hidden)
    active = values.astype(jnp.bfloat16)
    back_proj = jnp.einsum("nc,fc->nf", flat_g, weight_out, preferred_element_type=jnp.float32)
    grad_hidden = (back_proj * slopes).astype(jnp.bfloat16)
    grad_flat = (
        flat_g.astype(jnp.float32)
        + jnp.einsum("nf,cf->nc", grad_hidden, weight_in, preferred_element_type=jnp.float32)
    ).astype(jnp.bfloat16)
    sum_in = jnp.einsum("nc,nf->cf", flat_z, grad_hidden, preferred_element_type=jnp.float32)
    sum_out = jnp.einsum("nf,nc->fc", active, flat_g, preferred_element_type=jnp.float32)
    grad_mid = grad_flat.reshape(tile_rows, tile_cols, channels)
    padded = padded_2(grad_mid, (("row", 0), ("col", 1)), radius)
    kernel_wide = kernel.astype(jnp.float32)

    def sweep(row_off, state_pair):
        accumulated, kernel_sums = state_pair
        slab_rows = lax.dynamic_slice_in_dim(padded, 2 * radius - row_off, tile_rows, 0)
        tap_row = lax.dynamic_index_in_dim(kernel_wide, row_off, 0, keepdims=False)
        tap_sums = []
        source_rows = lax.dynamic_slice_in_dim(padded_in, row_off, tile_rows, 0)
        for offset in range(KS):
            shifted = slab_rows[:, 2 * radius - offset : 2 * radius - offset + tile_cols].astype(
                jnp.float32
            )
            accumulated = accumulated + tap_row[offset] * shifted
            tap_sums.append(
                jnp.sum(
                    source_rows[:, offset : offset + tile_cols].astype(jnp.float32)
                    * grad_mid.astype(jnp.float32),
                    axis=(0, 1),
                )
            )
        kernel_sums = lax.dynamic_update_index_in_dim(kernel_sums, jnp.stack(tap_sums), row_off, 0)
        return (accumulated, kernel_sums)

    start = (
        jnp.zeros((tile_rows, tile_cols, channels), jnp.float32),
        jnp.zeros((KS, KS, channels), jnp.float32),
    )
    accumulated, kernel_sums = lax.fori_loop(0, KS, sweep, start)
    grad_inputs = (grad_mid.astype(jnp.float32) + accumulated).astype(jnp.bfloat16)
    devices_all = lax.axis_size("row") * lax.axis_size("col")
    pixel_count = tile_rows * tile_cols * devices_all
    grad_scale = 1.0 / math.sqrt(pixel_count)
    total_in, total_out, total_kernel = lax.psum((sum_in, sum_out, kernel_sums), ("row", "col"))
    final_in = (total_in * grad_scale).astype(jnp.bfloat16)
    final_out = (total_out * grad_scale).astype(jnp.bfloat16)
    final_kernel = (total_kernel * grad_scale).astype(jnp.bfloat16)
    return (grad_inputs, final_in, final_out, final_kernel)


def solution(mesh):
    return jax.shard_map(
        per_device,
        mesh=mesh,
        in_specs=(
            P("row", "col", None),
            P("row", "col", None),
            P("row", "col", None),
            P(),
            P(),
            P(),
        ),
        out_specs=(P("row", "col", None), P(), P(), P()),
        check_vma=False,
    )
```

profile of v0, /device:TPU:8, one launch (start us, length us, event | category | flops | bytes accessed | tf_op | source)
XLA Modules:
  0.0 736.3 jit_solution(15265155077819901932)
XLA Ops:
  9.6 3.0 collective-permute-start.4
  16.3 3.8 collective-permute-start
  23.0 4.0 collective-permute-start.6
  27.0 9.4 %collective-permute-start.7 = (bf16[42,13,256]{2,1,0:T(8,128)(2,1)S(1)}, bf16[42,13,256]{2,1,0:T(8,128)(2,1)S(1)}, u32[]{:S(2)}, u32[]{:S(2)}) collective-permute-start(bf16[42,13,256]{2,1,0:T(8,128)(2,1)S(1)} %get-tuple-element.283), channel_id=1, source_target_pairs={{1,0},{2,1},{3,2},{4,3},{5,4},{6,5},{7,6},{8,7},{9,8},{10,9},{11,1... | collective-permute-start | bytes 838664 | tf_op jit(solution)/shard_map/ppermute | solution.py:20
  38.5 6.0 collective-permute-start.3
  46.4 4.6 collective-permute-done.2
  53.4 179.6 %while.18 = (s32[]{:T(128)}, f32[16,16,256]{2,1,0:T(8,128)S(1)}, f32[27,27,256]{2,1,0:T(8,128)}, f32[27,27,256]{2,1,0:T(8,128)}, bf16[42,42,256]{2,1,0:T(8,128)(...) while((s32[]{:T(128)}, f32[16,16,256]{2,1,0:T(8,128)S(1)}, ...), condition=%wide.region_28.29_spmd.clone, body=%wide.region_0.28_spmd.clone.sunk | while | flops 10806561 | bytes 8091653 | solution.py:80
  57.4 2.1 multiply_add_fusion.3
  64.0 2.1 multiply_add_fusion.3
  70.6 2.1 multiply_add_fusion.3
  77.4 2.1 multiply_add_fusion.3
  84.1 2.1 multiply_add_fusion.3
  90.7 2.1 multiply_add_fusion.3
  104.0 2.1 multiply_add_fusion.3
  117.3 2.1 multiply_add_fusion.3
  130.6 2.1 multiply_add_fusion.3
  143.9 2.1 multiply_add_fusion.3
  157.2 2.1 multiply_add_fusion.3
  170.4 2.1 multiply_add_fusion.3
  183.7 2.1 multiply_add_fusion.3
  197.0 2.1 multiply_add_fusion.3
  210.3 2.1 multiply_add_fusion.3
  223.6 2.1 multiply_add_fusion.3
  233.7 491.6 %all-reduce.3.cloned.1.call-done = (f32[256,1024]{0,1:T(8,128)}, f32[1024,256]{1,0:T(8,128)}, f32[27,27,256]{2,1,0:T(8,128)}) async-done(((f32[256,1024]{0,1:T(8,128)}, f32[1024,256]{1,0:T(8,128)}, f32[27,27,256]{2,1,0:T(8,128)}), (f32[256,1024]{0,1:T(8,128)}, f32[1024,256]{1,0:T(8,128)}, f32[27,27,256]{2,1,0:T(8,128)})) %all-reduce.3.cloned.1.call-update) | async-done | bytes 2843664 | tf_op jit(solution)/shard_map/psum | solution.py:85
  (224 shorter events, 165.7 us)
Async XLA Ops:
  7.2 5.5 copy-start
  7.2 6.7 copy-start.7
  7.2 6.7 copy-start.6
  7.2 718.1 %all-reduce.3.cloned.1.call-start = ((), (), s32[]{:S(2)}) async-start(), calls=%async_computation | async-start | bytes 5963776 | tf_op jit(solution)/shard_map/psum | solution.py:85
  8.3 14.5 %collective-permute-start.5 = (bf16[13,16,256]{2,1,0:T(8,128)(2,1)S(1)}, bf16[13,16,256]{2,1,0:T(8,128)(2,1)S(1)}, u32[]{:S(2)}, u32[]{:S(2)}) collective-permute-start(bf16[13,16,256]{2,1,0:T(8,128)(2,1)S(1)} %get-tuple-element.286), channel_id=1, source_target_pairs={{32,0},{64,32},{96,64},{128,96},{160,128},{192,160},{224,192},{256... | collective-permute-start | bytes 319496 | tf_op jit(solution)/shard_map/ppermute | solution.py:20
  9.6 13.1 %collective-permute-start.4 = (bf16[13,16,256]{2,1,0:T(8,128)(2,1)S(1)}, bf16[13,16,256]{2,1,0:T(8,128)(2,1)S(1)}, u32[]{:S(2)}, u32[]{:S(2)}) collective-permute-start(bf16[13,16,256]{2,1,0:T(8,128)(2,1)S(1)} %get-tuple-element.287), channel_id=1, source_target_pairs={{0,32},{32,64},{64,96},{96,128},{128,160},{160,192},{192,224},{224... | collective-permute-start | bytes 319496 | tf_op jit(solution)/shard_map/ppermute | solution.py:17
  15.0 21.3 %collective-permute-start.1 = (bf16[13,16,256]{2,1,0:T(8,128)(2,1)S(1)}, bf16[13,16,256]{2,1,0:T(8,128)(2,1)S(1)}, u32[]{:S(2)}, u32[]{:S(2)}) collective-permute-start(bf16[13,16,256]{2,1,0:T(8,128)(2,1)S(1)} %bitcast.191), channel_id=1, source_target_pairs={{32,0},{64,32},{96,64},{128,96},{160,128},{192,160},{224,192},{256... | collective-permute-start | bytes 319496 | tf_op jit(solution)/shard_map/ppermute | solution.py:20
  16.3 5.4 copy-start.5
  16.3 20.0 %collective-permute-start = (bf16[13,16,256]{2,1,0:T(8,128)(2,1)S(1)}, bf16[13,16,256]{2,1,0:T(8,128)(2,1)S(1)}, u32[]{:S(2)}, u32[]{:S(2)}) collective-permute-start(bf16[13,16,256]{2,1,0:T(8,128)(2,1)S(1)} %bitcast.190), channel_id=1, source_target_pairs={{0,32},{32,64},{64,96},{96,128},{128,160},{160,192},{192,224},{224... | collective-permute-start | bytes 319496 | tf_op jit(solution)/shard_map/ppermute | solution.py:17
  21.7 1.0 copy-start.2
  23.0 21.6 %copy-start.4 = (bf16[16,16,256]{2,1,0:T(8,128)(2,1)S(1)}, bf16[16,16,256]{2,1,0:T(8,128)(2,1)}, u32[]{:S(2)}) copy-start(bf16[16,16,256]{2,1,0:T(8,128)(2,1)} %param.9) | copy-start | bytes 393220
  23.0 23.0 %collective-permute-start.6 = (bf16[42,13,256]{2,1,0:T(8,128)(2,1)S(1)}, bf16[42,13,256]{2,1,0:T(8,128)(2,1)S(1)}, u32[]{:S(2)}, u32[]{:S(2)}) collective-permute-start(bf16[42,13,256]{2,1,0:T(8,128)(2,1)S(1)} %get-tuple-element.282), channel_id=1, source_target_pairs={{0,1},{1,2},{2,3},{3,4},{4,5},{5,6},{6,7},{7,8},{8,9},{9,10},{10,1... | collective-permute-start | bytes 838664 | tf_op jit(solution)/shard_map/ppermute | solution.py:17
  27.0 19.0 %collective-permute-start.7 = (bf16[42,13,256]{2,1,0:T(8,128)(2,1)S(1)}, bf16[42,13,256]{2,1,0:T(8,128)(2,1)S(1)}, u32[]{:S(2)}, u32[]{:S(2)}) collective-permute-start(bf16[42,13,256]{2,1,0:T(8,128)(2,1)S(1)} %get-tuple-element.283), channel_id=1, source_target_pairs={{1,0},{2,1},{3,2},{4,3},{5,4},{6,5},{7,6},{8,7},{9,8},{10,9},{11,1... | collective-permute-start | bytes 838664 | tf_op jit(solution)/shard_map/ppermute | solution.py:20
  36.6 14.5 %collective-permute-start.2 = (bf16[42,13,256]{2,1,0:T(8,128)(2,1)S(1)}, bf16[42,13,256]{2,1,0:T(8,128)(2,1)S(1)}, u32[]{:S(2)}, u32[]{:S(2)}) collective-permute-start(bf16[42,13,256]{2,1,0:T(8,128)(2,1)S(1)} %get-tuple-element.284), channel_id=1, source_target_pairs={{0,1},{1,2},{2,3},{3,4},{4,5},{5,6},{6,7},{7,8},{8,9},{9,10},{10,1... | collective-permute-start | bytes 838664 | tf_op jit(solution)/shard_map/ppermute | solution.py:17
  38.5 14.5 %collective-permute-start.3 = (bf16[42,13,256]{2,1,0:T(8,128)(2,1)S(1)}, bf16[42,13,256]{2,1,0:T(8,128)(2,1)S(1)}, u32[]{:S(2)}, u32[]{:S(2)}) collective-permute-start(bf16[42,13,256]{2,1,0:T(8,128)(2,1)S(1)} %get-tuple-element.285), channel_id=1, source_target_pairs={{1,0},{2,1},{3,2},{4,3},{5,4},{6,5},{7,6},{8,7},{9,8},{10,9},{11,1... | collective-permute-start | bytes 838664 | tf_op jit(solution)/shard_map/ppermute | solution.py:20
  725.3 2.4 copy-start.3
  726.7 1.9 copy-start.1
Sparse Core Ops, SparseCore 0:
  233.1 492.1 all-reduce.2
where the time goes:
time: 740 us; the launch traced here: 736 us
  waiting for transfers between devices  498 us (67%)
  other arithmetic  110 us (15%)
  local copies, waits for them, and re-layouts  77.1 us (10%)
  starting transfers between devices  30.7 us (4%)
  between operations  14.3 us (2%)
    psum x1, waiting for transfers between devices, per_device(): lax.psum((sum_in, sum_out, kernel_sums), ('row', 'col'))  492 us
    add x27, other arithmetic, sweep(): accumulated = accumulated + tap_row[offset] * shifted  56.6 us
    slice x54, local copies, waits for them, and re-layouts, sweep(): accumulated = accumulated + tap_row[offset] * shifted  55.3 us
    reduce_sum x54, other arithmetic, sweep(): jnp.sum(source_rows[:, offset:offset + tile_cols].astype(jnp.float32) * g...  47.9 us
    ppermute x4, starting transfers between devices, padded_2(): lax.ppermute(lax.slice_in_dim(block, 0, width, axis=dim), axis, backward)  18 us
    dynamic_update_slice x27, local copies, waits for them, and re-layouts, sweep(): lax.dynamic_update_index_in_dim(kernel_sums, jnp.stack(tap_sums), row_off...  16.5 us
  transfers between devices with their start and end apart: 9, of which 3 were waited for; matrix products, arithmetic and copies ran while one was open for 1% of the time, Pallas kernels for 0%

commit v1 on v0

--- a/solution.py
+++ b/solution.py
@@ -82,7 +82,9 @@
     devices_all = lax.axis_size("row") * lax.axis_size("col")
     pixel_count = tile_rows * tile_cols * devices_all
     grad_scale = 1.0 / math.sqrt(pixel_count)
-    total_in, total_out, total_kernel = lax.psum((sum_in, sum_out, kernel_sums), ("row", "col"))
+    total_in, total_out, total_kernel = lax.psum(
+        lax.psum((sum_in, sum_out, kernel_sums), "row"), "col"
+    )
     final_in = (total_in * grad_scale).astype(jnp.bfloat16)
     final_out = (total_out * grad_scale).astype(jnp.bfloat16)
     final_kernel = (total_kernel * grad_scale).astype(jnp.bfloat16)

time: 740 us -> 684 us (0.924)
  the two profiles are of different devices: /device:TPU:8 before, /device:TPU:2 now
where the time goes in v1:
time: 684 us; the launch traced here: 680 us
  waiting for transfers between devices  450 us (66%)
  other arithmetic  110 us (16%)
  local copies, waits for them, and re-layouts  77.1 us (11%)
  starting transfers between devices  22.5 us (3%)
  between operations  14.3 us (2%)
    psum x1, waiting for transfers between devices, per_device(): lax.psum(lax.psum((sum_in, sum_out, kernel_sums), 'row'), 'col')  277 us
    psum x1, waiting for transfers between devices, per_device(): lax.psum((sum_in, sum_out, kernel_sums), 'row')  164 us
    add x27, other arithmetic, sweep(): accumulated = accumulated + tap_row[offset] * shifted  56.6 us
    slice x54, local copies, waits for them, and re-layouts, sweep(): accumulated = accumulated + tap_row[offset] * shifted  55.3 us
    reduce_sum x54, other arithmetic, sweep(): jnp.sum(source_rows[:, offset:offset + tile_cols].astype(jnp.float32) * g...  47.9 us
    dynamic_update_slice x27, local copies, waits for them, and re-layouts, sweep(): lax.dynamic_update_index_in_dim(kernel_sums, jnp.stack(tap_sums), row_off...  16.5 us
  transfers between devices with their start and end apart: 10, of which 5 were waited for; matrix products, arithmetic and copies ran while one was open for 1% of the time, Pallas kernels for 0%

profile of v1, /device:TPU:2, one launch (start us, length us, event | category | flops | bytes accessed | tf_op | source)
XLA Modules:
  0.0 680.1 jit_solution(1632951990375004131)
XLA Ops:
  10.2 2.4 collective-permute-start.4
  15.0 7.4 %collective-permute-start.1 = (bf16[13,16,256]{2,1,0:T(8,128)(2,1)S(1)}, bf16[13,16,256]{2,1,0:T(8,128)(2,1)S(1)}, u32[]{:S(2)}, u32[]{:S(2)}) collective-permute-start(bf16[13,16,256]{2,1,0:T(8,128)(2,1)S(1)} %bitcast.191), channel_id=1, source_target_pairs={{32,0},{64,32},{96,64},{128,96},{160,128},{192,160},{224,192},{256... | collective-permute-start | bytes 319496 | tf_op jit(solution)/shard_map/ppermute | solution.py:20
  30.3 4.6 collective-permute-start.2
  37.6 4.0 collective-permute-done.7
  43.5 4.3 collective-permute-done.3
  48.2 179.6 %while.18 = (s32[]{:T(128)}, f32[16,16,256]{2,1,0:T(8,128)S(1)}, f32[27,27,256]{2,1,0:T(8,128)}, f32[27,27,256]{2,1,0:T(8,128)}, bf16[42,42,256]{2,1,0:T(8,128)(...) while((s32[]{:T(128)}, f32[16,16,256]{2,1,0:T(8,128)S(1)}, ...), condition=%wide.region_28.29_spmd.clone, body=%wide.region_0.28_spmd.clone.sunk | while | flops 10806561 | bytes 8091653 | solution.py:80
  58.9 2.1 multiply_add_fusion.3
  65.5 2.1 multiply_add_fusion.3
  72.3 2.1 multiply_add_fusion.3
  78.9 2.1 multiply_add_fusion.3
  85.6 2.1 multiply_add_fusion.3
  98.9 2.1 multiply_add_fusion.3
  105.5 2.1 multiply_add_fusion.3
  112.1 2.1 multiply_add_fusion.3
  125.4 2.1 multiply_add_fusion.3
  138.7 2.1 multiply_add_fusion.3
  152.0 2.1 multiply_add_fusion.3
  165.3 2.1 multiply_add_fusion.3
  178.6 2.1 multiply_add_fusion.3
  191.9 2.1 multiply_add_fusion.3
  205.2 2.1 multiply_add_fusion.3
  218.4 2.1 multiply_add_fusion.3
  227.9 163.8 %all-reduce.7.cloned.1.call-done = (f32[256,1024]{0,1:T(8,128)}, f32[1024,256]{1,0:T(8,128)}, f32[27,27,256]{2,1,0:T(8,128)}) async-done(((f32[256,1024]{0,1:T(8,128)}, f32[1024,256]{1,0:T(8,128)}, f32[27,27,256]{2,1,0:T(8,128)}), (f32[256,1024]{0,1:T(8,128)}, f32[1024,256]{1,0:T(8,128)}, f32[27,27,256]{2,1,0:T(8,128)})) %all-reduce.7.cloned.1.call-update) | async-done | bytes 2843664 | tf_op jit(solution)/shard_map/psum | solution.py:86
  392.3 276.8 %all-reduce.5.cloned.1.call-done = (f32[256,1024]{0,1:T(8,128)}, f32[1024,256]{1,0:T(8,128)}, f32[27,27,256]{2,1,0:T(8,128)}) async-done(((f32[256,1024]{0,1:T(8,128)}, f32[1024,256]{1,0:T(8,128)}, f32[27,27,256]{2,1,0:T(8,128)}), (f32[256,1024]{0,1:T(8,128)}, f32[1024,256]{1,0:T(8,128)}, f32[27,27,256]{2,1,0:T(8,128)})) %all-reduce.5.cloned.1.call-update) | async-done | bytes 2843664 | tf_op jit(solution)/shard_map/psum | solution.py:85
  (227 shorter events, 168.7 us)
Async XLA Ops:
  7.2 5.5 copy-start
  7.2 6.7 copy-start.7
  7.2 6.7 copy-start.6
  7.2 384.4 %all-reduce.7.cloned.1.call-start = ((), (), s32[]{:S(2)}) async-start(), calls=%async_computation.1 | async-start | bytes 5963776 | tf_op jit(solution)/shard_map/psum | solution.py:86
  8.3 18.9 %collective-permute-start.5 = (bf16[13,16,256]{2,1,0:T(8,128)(2,1)S(1)}, bf16[13,16,256]{2,1,0:T(8,128)(2,1)S(1)}, u32[]{:S(2)}, u32[]{:S(2)}) collective-permute-start(bf16[13,16,256]{2,1,0:T(8,128)(2,1)S(1)} %get-tuple-element.289), channel_id=1, source_target_pairs={{32,0},{64,32},{96,64},{128,96},{160,128},{192,160},{224,192},{256... | collective-permute-start | bytes 319496 | tf_op jit(solution)/shard_map/ppermute | solution.py:20
  10.2 16.9 %collective-permute-start.4 = (bf16[13,16,256]{2,1,0:T(8,128)(2,1)S(1)}, bf16[13,16,256]{2,1,0:T(8,128)(2,1)S(1)}, u32[]{:S(2)}, u32[]{:S(2)}) collective-permute-start(bf16[13,16,256]{2,1,0:T(8,128)(2,1)S(1)} %get-tuple-element.290), channel_id=1, source_target_pairs={{0,32},{32,64},{64,96},{96,128},{128,160},{160,192},{192,224},{224... | collective-permute-start | bytes 319496 | tf_op jit(solution)/shard_map/ppermute | solution.py:17
  15.0 15.1 %collective-permute-start.1 = (bf16[13,16,256]{2,1,0:T(8,128)(2,1)S(1)}, bf16[13,16,256]{2,1,0:T(8,128)(2,1)S(1)}, u32[]{:S(2)}, u32[]{:S(2)}) collective-permute-start(bf16[13,16,256]{2,1,0:T(8,128)(2,1)S(1)} %bitcast.191), channel_id=1, source_target_pairs={{32,0},{64,32},{96,64},{128,96},{160,128},{192,160},{224,192},{256... | collective-permute-start | bytes 319496 | tf_op jit(solution)/shard_map/ppermute | solution.py:20
  22.5 3.7 copy-start.5
  22.5 7.7 %collective-permute-start = (bf16[13,16,256]{2,1,0:T(8,128)(2,1)S(1)}, bf16[13,16,256]{2,1,0:T(8,128)(2,1)S(1)}, u32[]{:S(2)}, u32[]{:S(2)}) collective-permute-start(bf16[13,16,256]{2,1,0:T(8,128)(2,1)S(1)} %bitcast.190), channel_id=1, source_target_pairs={{0,32},{32,64},{64,96},{96,128},{128,160},{160,192},{192,224},{224... | collective-permute-start | bytes 319496 | tf_op jit(solution)/shard_map/ppermute | solution.py:17
  26.1 1.0 copy-start.2
  27.4 8.9 %copy-start.4 = (bf16[16,16,256]{2,1,0:T(8,128)(2,1)S(1)}, bf16[16,16,256]{2,1,0:T(8,128)(2,1)}, u32[]{:S(2)}) copy-start(bf16[16,16,256]{2,1,0:T(8,128)(2,1)} %param.9) | copy-start | bytes 393220
  27.4 10.2 %collective-permute-start.6 = (bf16[42,13,256]{2,1,0:T(8,128)(2,1)S(1)}, bf16[42,13,256]{2,1,0:T(8,128)(2,1)S(1)}, u32[]{:S(2)}, u32[]{:S(2)}) collective-permute-start(bf16[42,13,256]{2,1,0:T(8,128)(2,1)S(1)} %get-tuple-element.285), channel_id=1, source_target_pairs={{0,1},{1,2},{2,3},{3,4},{4,5},{5,6},{6,7},{7,8},{8,9},{9,10},{10,1... | collective-permute-start | bytes 838664 | tf_op jit(solution)/shard_map/ppermute | solution.py:17
  28.8 12.8 %collective-permute-start.7 = (bf16[42,13,256]{2,1,0:T(8,128)(2,1)S(1)}, bf16[42,13,256]{2,1,0:T(8,128)(2,1)S(1)}, u32[]{:S(2)}, u32[]{:S(2)}) collective-permute-start(bf16[42,13,256]{2,1,0:T(8,128)(2,1)S(1)} %get-tuple-element.286), channel_id=1, source_target_pairs={{1,0},{2,1},{3,2},{4,3},{5,4},{6,5},{7,6},{8,7},{9,8},{10,9},{11,1... | collective-permute-start | bytes 838664 | tf_op jit(solution)/shard_map/ppermute | solution.py:20
  30.3 13.2 %collective-permute-start.2 = (bf16[42,13,256]{2,1,0:T(8,128)(2,1)S(1)}, bf16[42,13,256]{2,1,0:T(8,128)(2,1)S(1)}, u32[]{:S(2)}, u32[]{:S(2)}) collective-permute-start(bf16[42,13,256]{2,1,0:T(8,128)(2,1)S(1)} %get-tuple-element.287), channel_id=1, source_target_pairs={{0,1},{1,2},{2,3},{3,4},{4,5},{5,6},{6,7},{7,8},{8,9},{9,10},{10,1... | collective-permute-start | bytes 838664 | tf_op jit(solution)/shard_map/ppermute | solution.py:17
  34.9 12.9 %collective-permute-start.3 = (bf16[42,13,256]{2,1,0:T(8,128)(2,1)S(1)}, bf16[42,13,256]{2,1,0:T(8,128)(2,1)S(1)}, u32[]{:S(2)}, u32[]{:S(2)}) collective-permute-start(bf16[42,13,256]{2,1,0:T(8,128)(2,1)S(1)} %get-tuple-element.288), channel_id=1, source_target_pairs={{1,0},{2,1},{3,2},{4,3},{5,4},{6,5},{7,6},{8,7},{9,8},{10,9},{11,1... | collective-permute-start | bytes 838664 | tf_op jit(solution)/shard_map/ppermute | solution.py:20
  227.8 441.3 %all-reduce.5.cloned.1.call-start = ((), (), s32[]{:S(2)}) async-start(), calls=%async_computation | async-start | bytes 5963776 | tf_op jit(solution)/shard_map/psum | solution.py:85
  669.1 2.4 copy-start.3
  670.5 1.9 copy-start.1
Sparse Core Ops, SparseCore 0:
  227.9 163.6 all-reduce.6
  394.8 274.2 all-reduce.4
